TPU v7x, 256 devices: a whole 4x4x8 slice. The times are simulated.
256 devices in a mesh: seq: 64 (over z, y, core), grp: 4 (over x).
Axes of the slice: x: 4, y: 4, z: 8, core: 2. Of those that a mesh axis runs over, the one named last changes fastest.
Arguments:
- q_nope: bfloat16 [1024, 128, 128], P('seq', 'grp'), may hold values from -6 to 6
- q_rope: bfloat16 [1024, 128, 64], P('seq', 'grp'), may hold values from -256 to 256
- cache: bfloat16 [65536, 576], P('seq'), may hold values from -6 to 6
- w_uk: bfloat16 [128, 65536], P('grp', 'seq'), may hold values from -0.5 to 0.5
- w_uv: bfloat16 [128, 65536], P('grp', 'seq'), may hold values from -0.25 to 0.25
- d_out: bfloat16 [1024, 128, 128], P('seq', 'grp'), may hold values from -6 to 6
- sel: int32 [1024, 32], P('seq'), may hold values from 0 to 63, as said below
- slot_blocks: int32 [64, 64], P('seq'), may hold values from 0 to 15, as said below
Outputs:
- attn_out: bfloat16 [1024, 128, 128], P('seq', 'grp')
- d_q_nope: bfloat16 [1024, 128, 128], P('seq', 'grp')
- d_q_rope: bfloat16 [1024, 128, 64], P('seq', 'grp')
- d_cache: float32 [65536, 576], P('seq')
Inputs may be any that keep to these rules, and one draw needn't show every extreme that they name: `sel`: each row names 32 different places; place s stands for the block that the row's device asks of device s. `slot_blocks`: entry [r, s] is the index among device s's own blocks of the block that device r asks for in place s; the 1 entries of a row toward one device differ.
All inputs are finite; a program needn't handle non-finite values.
Results may differ from a plain program's by a relative error of at most 0.015.
Values may be sent and summed in bfloat16 or wider, within the bound.
A program may use at most 128 MiB of HBM per device.

v0:
```python
import math
import jax
import jax.numpy as jnp
from jax import lax
from jax.sharding import PartitionSpec as P

BLOCK_LEN = 64


def local(q_nope, q_rope, cache, w_uk, w_uv, d_out, sel, slot_blocks):
    peers = lax.axis_size("seq")
    queries, heads, nope = q_nope.shape
    rope = q_rope.shape[2]
    width = cache.shape[1]
    latent = width - rope
    value = d_out.shape[2]
    slot_total = slot_blocks.shape[1]
    per_peer = slot_total // peers
    own_blocks = cache.shape[0] // BLOCK_LEN
    scale = 1.0 / math.sqrt(nope + rope)
    gathered_k, gathered_v = (
        lax.all_gather(w_uk, "seq", axis=1, tiled=True),
        lax.all_gather(w_uv, "seq", axis=1, tiled=True),
    )
    weight_k = gathered_k.reshape(heads, nope, latent)
    weight_v = gathered_v.reshape(heads, latent, value)
    wanted = slot_blocks.reshape(peers, per_peer)
    asked = lax.all_to_all(wanted, "seq", split_axis=0, concat_axis=0, tiled=True)
    blocks = cache.reshape(own_blocks, BLOCK_LEN, width)
    arrived = lax.all_to_all(blocks[asked], "seq", split_axis=0, concat_axis=0, tiled=True)
    keys = arrived.reshape(slot_total * BLOCK_LEN, width)
    keys_lat = keys[:, :latent]
    q_lat = jnp.einsum("qhn,hnl->qhl", q_nope, weight_k, preferred_element_type=jnp.float32).astype(
        jnp.bfloat16
    )
    qfull = jnp.concatenate([q_lat, q_rope], axis=-1)
    chosen = jnp.any(
        sel[:, :, None] == jnp.arange(slot_total, dtype=jnp.int32)[None, None, :], axis=1
    )
    live = jnp.repeat(chosen, BLOCK_LEN, axis=1)[:, None, :]
    score = jnp.einsum("qhc,tc->qht", qfull, keys, preferred_element_type=jnp.float32) * scale
    score = jnp.where(live, score, -jnp.inf)
    prob = jax.nn.softmax(score, axis=-1)
    prob_low = prob.astype(jnp.bfloat16)
    olat = jnp.einsum("qht,tl->qhl", prob_low, keys_lat, preferred_element_type=jnp.float32).astype(
        jnp.bfloat16
    )
    attn_out = jnp.einsum(
        "qhl,hlv->qhv", olat, weight_v, preferred_element_type=jnp.float32
    ).astype(jnp.bfloat16)
    d_olat = jnp.einsum("qhv,hlv->qhl", d_out, weight_v, preferred_element_type=jnp.float32).astype(
        jnp.bfloat16
    )
    dprob = jnp.einsum("qhl,tl->qht", d_olat, keys_lat, preferred_element_type=jnp.float32)
    delta = jnp.sum(prob * dprob, axis=-1, keepdims=True)
    dscore = (prob * (dprob - delta) * scale).astype(jnp.bfloat16)
    dquery = jnp.einsum("qht,tc->qhc", dscore, keys, preferred_element_type=jnp.float32)
    d_q_rope = dquery[:, :, latent:].astype(jnp.bfloat16)
    d_qlat = dquery[:, :, :latent].astype(jnp.bfloat16)
    d_q_nope = jnp.einsum(
        "qhl,hnl->qhn", d_qlat, weight_k, preferred_element_type=jnp.float32
    ).astype(jnp.bfloat16)
    value_part = jnp.einsum("qht,qhl->tl", prob_low, d_olat, preferred_element_type=jnp.float32)
    dkeys = jnp.einsum("qht,qhc->tc", dscore, qfull, preferred_element_type=jnp.float32)
    dkeys = dkeys + jnp.pad(value_part, ((0, 0), (0, rope)))
    one_hot = (
        asked.reshape(-1)[:, None] == jnp.arange(own_blocks, dtype=jnp.int32)[None, :]
    ).astype(jnp.float32)
    returned = lax.all_to_all(
        dkeys.reshape(peers, per_peer, BLOCK_LEN * width).astype(jnp.bfloat16),
        "seq",
        split_axis=0,
        concat_axis=0,
        tiled=True,
    ).astype(jnp.float32)
    local_grad = jnp.dot(
        one_hot.T,
        returned.reshape(peers * per_peer, BLOCK_LEN * width),
        precision=lax.Precision.HIGHEST,
    )
    d_cache = (
        lax.psum(local_grad.astype(jnp.bfloat16), "grp")
        .astype(jnp.float32)
        .reshape(own_blocks * BLOCK_LEN, width)
    )
    return (attn_out, d_q_nope, d_q_rope, d_cache)


def solution(mesh):
    return jax.shard_map(
        local,
        mesh=mesh,
        in_specs=(
            P("seq", "grp", None),
            P("seq", "grp", None),
            P("seq", None),
            P("grp", "seq"),
            P("grp", "seq"),
            P("seq", "grp", None),
            P("seq", None),
            P("seq", None),
        ),
        out_specs=(
            P("seq", "grp", None),
            P("seq", "grp", None),
            P("seq", "grp", None),
            P("seq", None),
        ),
        check_vma=False,
    )
```

profile of v0, /device:TPU:8, one launch (start us, length us, event | category | flops | bytes accessed | tf_op | source)
XLA Modules:
  0.0 523.4 jit_solution(6179962597997448510)
XLA Ops:
  9.3 12.1 %all-to-all-start = ((s32[64,1,1]{2,1,0:T(1,128)}), s32[64,1,1]{2,1,0:T(1,128)S(1)}, u32[]{:S(2)}, u32[]{:S(2)}) async-start(s32[64,1,1]{2,1,0:T(1,128)} %copy.80), calls=%async_computation | async-start | bytes 65536 | tf_op jit(solution)/shard_map/all_to_all | solution.py:28
  23.1 6.9 %all-to-all-done = s32[64,1,1]{2,1,0:T(1,128)S(1)} async-done(((s32[64,1,1]{2,1,0:T(1,128)}), s32[64,1,1]{2,1,0:T(1,128)S(1)}, u32[]{:S(2)}, u32[]{:S(2)}) %all-to-all-start) | async-done | bytes 288 | tf_op jit(solution)/shard_map/all_to_all | solution.py:28
  32.3 3.5 gather_fusion
  35.8 6.7 %all-to-all-start.1 = ((bf16[64,1,64,576]{3,2,1,0:T(8,128)(2,1)}), bf16[64,1,64,576]{3,2,1,0:T(8,128)(2,1)}, u32[]{:S(2)}, u32[]{:S(2)}) async-start(bf16[64,1,64,576]{3,2,1,0:T(8,128)(2,1)} %bitcast.47), calls=%async_computation.1 | async-start | bytes 10485760 | tf_op jit(solution)/shard_map/all_to_all | solution.py:30
  43.9 67.8 %all-gather.5.cloned.1.call-done = bf16[32,65536]{1,0:T(8,128)(2,1)} async-done(((bf16[32,1024]{1,0:T(8,128)(2,1)}), bf16[32,65536]{1,0:T(8,128)(2,1)}) %all-gather.5.cloned.1.call-update) | async-done | bytes 4194320 | tf_op jit(solution)/shard_map/all_gather | solution.py:23
  111.7 5.1 copy.102
  116.8 78.3 %all-gather.3.cloned.1.call-done = bf16[32,65536]{1,0:T(8,128)(2,1)} async-done(((bf16[32,1024]{1,0:T(8,128)(2,1)}), bf16[32,65536]{1,0:T(8,128)(2,1)}) %all-gather.3.cloned.1.call-update) | async-done | bytes 4194320 | tf_op jit(solution)/shard_map/all_gather | solution.py:22
  195.1 3.9 copy.101
  203.0 8.0 %fusion.12 = f32[16,32,4096]{2,1,0:T(8,128)} fusion(bf16[4096,576]{1,0:T(8,128)(2,1)} %bitcast.5, bf16[16,32,512]{2,0,1:T(8,128)(2,1)S(1)} %fusion.27), kind=kOutput, calls=%fused_computation.20 | convolution fusion | flops 2147483648 | bytes 13107200 | tf_op jit(solution)/shard_map/qhl,tl->qht/dot_general | solution.py:54
  211.0 10.7 %fusion.50 = (f32[16,32]{1,0:T(8,128)S(1)}, f32[16,32,4096]{2,1,0:T(8,128)}) fusion(pred[16,4096]{1,0:T(8,128)(4,1)S(1)} %broadcast_in_dim.25, bf16[4096,576,1]{1,0,2:T(8,128)(2,1)} %bitcast.6, bf16[16,32,576]{2,0,1:T(8,128)(2,1)S(1)} %pad_maximum_fusion), kind=kOutput, calls=%fused_computation.59 | convolution fusion | flops 2424311808 | bytes 13764608 | tf_op jit(solution)/shard_map/sub | solution.py:43
  221.7 9.4 %convolution_bitcast_fusion = f32[4096,512]{0,1:T(8,128)} fusion(bf16[16,32,512]{2,0,1:T(8,128)(2,1)S(1)} %fusion.27, f32[16,32,4096]{2,1,0:T(8,128)} %get-tuple-element.27, f32[16,32]{1,0:T(8,128)S(1)} %get-tuple-element.26), kind=kOutput, calls=%fused_computation.12 | convolution fusion | flops 2151677952 | bytes 17303552 | tf_op jit(solution)/shard_map/qht,qhl->tl/dot_general | solution.py:63
  231.1 18.8 %fusion.2 = bf16[4096,576]{0,1:T(8,128)(2,1)} fusion(f32[4096,512]{0,1:T(8,128)} %convolution_bitcast_fusion, f32[16,32,4096]{2,1,0:T(8,128)} %fusion.12, bf16[16,32,576]{2,0,1:T(8,128)(2,1)S(1)} %pad_maximum_fusion, f32[16,32,4096]{2,1,0:T(8,128)} %get-tuple-element.27, f32[16,32]{1,0:T(8,128)S(1)} %get-tuple-element.26), kind=kOutput, calls=%fused_computation.5 | convolution fusion | flops 2435322368 | bytes 30476288 | tf_op jit(solution)/shard_map/qht,qhc->tc/dot_general | solution.py:64
  249.9 7.6 %copy.91 = bf16[4096,576]{1,0:T(8,128)(2,1)} copy(bf16[4096,576]{0,1:T(8,128)(2,1)} %fusion.2) | data formatting | bytes 9437184 | tf_op jit(solution)/shard_map/convert_element_type | solution.py:70
  257.5 21.7 %convert_element_type.71 = bf16[64,1,36864]{2,1,0:T(2,128)(2,1)} reshape(bf16[4096,576]{1,0:T(8,128)(2,1)} %copy.91) | data formatting | bytes 9437184 | tf_op jit(solution)/shard_map/convert_element_type | solution.py:70
  279.7 29.9 %reduce.4 = bf16[64,36864]{1,0:T(8,128)(2,1)} reduce(bf16[64,1,36864]{2,1,0:T(2,128)(2,1)} %convert_element_type.71, bf16[]{:T(256)} %broadcast.36), dimensions={1}, to_apply=%convert_element_type.71.reduce_sub_computation | reduce | bytes 9437186 | tf_op jit(solution)/shard_map/convert_element_type | solution.py:70
  309.7 8.3 %reshape.84 = bf16[64,2,18432]{2,1,0:T(2,128)(2,1)} reshape(bf16[64,36864]{1,0:T(8,128)(2,1)} %reduce.4) | data formatting | bytes 9437184
  317.9 8.0 %all-to-all-start.2 = ((bf16[64,2,18432]{2,1,0:T(2,128)(2,1)}), bf16[64,2,18432]{2,1,0:T(2,128)(2,1)}, u32[]{:S(2)}, u32[]{:S(2)}) async-start(bf16[64,2,18432]{2,1,0:T(2,128)(2,1)} %reshape.84), calls=%async_computation.2 | async-start | bytes 9437184 | tf_op jit(solution)/shard_map/all_to_all | solution.py:69
  326.2 7.0 %fusion.24 = bf16[16,32,512]{2,1,0:T(8,128)(2,1)S(1)} fusion(bf16[4096,576]{1,0:T(8,128)(2,1)} %bitcast.5, f32[16,32,4096]{2,1,0:T(8,128)} %get-tuple-element.27, f32[16,32]{1,0:T(8,128)S(1)} %get-tuple-element.26), kind=kOutput, calls=%fused_computation.26 | convolution fusion | flops 2151940096 | bytes 13109248 | tf_op jit(solution)/shard_map/qht,tl->qhl/dot_general | solution.py:45
  333.2 100.1 %all-to-all-done.2 = bf16[64,2,18432]{2,1,0:T(2,128)(2,1)} async-done(((bf16[64,2,18432]{2,1,0:T(2,128)(2,1)}), bf16[64,2,18432]{2,1,0:T(2,128)(2,1)}, u32[]{:S(2)}, u32[]{:S(2)}) %all-to-all-start.2) | async-done | bytes 4718624 | tf_op jit(solution)/shard_map/all_to_all | solution.py:69
  433.3 20.2 %reshape.85 = bf16[64,1,36864]{2,1,0:T(2,128)(2,1)} reshape(bf16[64,2,18432]{2,1,0:T(2,128)(2,1)} %all-to-all-done.2) | data formatting | bytes 9437184
  453.4 8.8 %convolution_convert_fusion = bf16[16,36864]{1,0:T(8,128)(2,1)S(1)} fusion(bf16[64,1,36864]{2,1,0:T(2,128)(2,1)} %reshape.85, s32[64]{0:T(128)S(1)} %get-tuple-element.24), kind=kOutput, calls=%fused_computation.3 | convolution fusion | flops 76088320 | bytes 5898496 | tf_op jit(solution)/shard_map/dot_general | solution.py:76
  464.7 14.8 %fusion.21 = bf16[16,32,576]{2,1,0:T(8,128)(2,1)S(1)} fusion(bf16[4096,576,1]{1,0,2:T(8,128)(2,1)} %bitcast.6, f32[16,32,4096]{2,1,0:T(8,128)} %fusion.12, f32[16,32,4096]{2,1,0:T(8,128)} %get-tuple-element.27, f32[16,32]{1,0:T(8,128)S(1)} %get-tuple-element.26), kind=kOutput, calls=%fused_computation.25 | convolution fusion | flops 2430898688 | bytes 22087680 | tf_op jit(solution)/shard_map/qht,tc->qhc/dot_general | solution.py:57
  480.2 3.5 fusion.29
  486.3 27.6 %all-reduce.3.cloned.1.call-done = bf16[1024,576]{1,0:T(8,128)(2,1)} async-done(((bf16[1024,576]{1,0:T(8,128)(2,1)}), bf16[1024,576]{1,0:T(8,128)(2,1)}) %all-reduce.3.cloned.1.call-update) | async-done | bytes 1179664 | tf_op jit(solution)/shard_map/psum | solution.py:82
  (42 shorter events, 20.8 us)
Async XLA Ops:
  7.2 194.6 %copy-start = (bf16[16,32,128]{2,1,0:T(8,128)(2,1)S(1)}, bf16[16,32,128]{2,1,0:T(8,128)(2,1)}, u32[]{:S(2)}) copy-start(bf16[16,32,128]{2,1,0:T(8,128)(2,1)} %param.13) | copy-start | bytes 393220
  7.2 104.5 %all-gather.5.cloned.1.call-start = ((), (), s32[]{:S(2)}) async-start(), calls=%async_computation.4 | async-start | bytes 4259840 | tf_op jit(solution)/shard_map/all_gather | solution.py:23
  9.3 20.7 %all-to-all-start = ((s32[64,1,1]{2,1,0:T(1,128)}), s32[64,1,1]{2,1,0:T(1,128)S(1)}, u32[]{:S(2)}, u32[]{:S(2)}) async-start(s32[64,1,1]{2,1,0:T(1,128)} %copy.80), calls=%async_computation | async-start | bytes 65536 | tf_op jit(solution)/shard_map/all_to_all | solution.py:28
  35.8 7.4 %copy-start.7 = (s32[16,32]{1,0:T(8,128)S(1)}, s32[16,32]{1,0:T(8,128)}, u32[]{:S(2)}) copy-start(s32[16,32]{1,0:T(8,128)} %param.14) | copy-start | bytes 6148
  35.8 8.0 %copy-start.6 = (bf16[16,32,64]{2,1,0:T(8,128)(2,1)S(1)}, bf16[16,32,64]{2,1,0:T(8,128)(2,1)}, u32[]{:S(2)}) copy-start(bf16[16,32,64]{2,1,0:T(8,128)(2,1)} %param.9) | copy-start | bytes 196612
  35.8 167.2 %all-to-all-start.1 = ((bf16[64,1,64,576]{3,2,1,0:T(8,128)(2,1)}), bf16[64,1,64,576]{3,2,1,0:T(8,128)(2,1)}, u32[]{:S(2)}, u32[]{:S(2)}) async-start(bf16[64,1,64,576]{3,2,1,0:T(8,128)(2,1)} %bitcast.47), calls=%async_computation.1 | async-start | bytes 10485760 | tf_op jit(solution)/shard_map/all_to_all | solution.py:30
  42.5 152.7 %all-gather.3.cloned.1.call-start = ((), (), s32[]{:S(2)}) async-start(), calls=%async_computation.3 | async-start | bytes 4259840 | tf_op jit(solution)/shard_map/all_gather | solution.py:22
  116.8 84.3 %copy-start.5 = (bf16[16,32,128]{2,1,0:T(8,128)(2,1)S(1)}, bf16[16,32,128]{2,1,0:T(8,128)(2,1)}, u32[]{:S(2)}) copy-start(bf16[16,32,128]{2,1,0:T(8,128)(2,1)} %param.8) | copy-start | bytes 393220
  195.1 6.7 %copy-start.2 = (bf16[4,8,512,128]{3,2,1,0:T(8,128)(2,1)S(1)}, bf16[4,8,512,128]{3,2,1,0:T(8,128)(2,1)}, u32[]{:S(2)}) copy-start(bf16[4,8,512,128]{3,2,1,0:T(8,128)(2,1)} %copy.102) | copy-start | bytes 12582916
  199.0 2.1 copy-start.3
  317.9 115.3 %all-to-all-start.2 = ((bf16[64,2,18432]{2,1,0:T(2,128)(2,1)}), bf16[64,2,18432]{2,1,0:T(2,128)(2,1)}, u32[]{:S(2)}, u32[]{:S(2)}) async-start(bf16[64,2,18432]{2,1,0:T(2,128)(2,1)} %reshape.84), calls=%async_computation.2 | async-start | bytes 9437184 | tf_op jit(solution)/shard_map/all_to_all | solution.py:69
  325.9 188.0 %all-reduce.3.cloned.1.call-start = ((), (), s32[]{:S(2)}) async-start(), calls=%async_computation.5 | async-start | bytes 2621440 | tf_op jit(solution)/shard_map/psum | solution.py:82
  479.5 5.0 copy-start.4
  480.2 36.4 %copy-start.1 = (bf16[16,32,128]{2,1,0:T(8,128)(2,1)S(1)}, bf16[16,32,128]{2,1,0:T(8,128)(2,1)}, u32[]{:S(2)}) copy-start(bf16[16,32,128]{2,1,0:T(8,128)(2,1)} %param.13) | copy-start | bytes 393220
Sparse Core Ops, SparseCore 0:
  10.8 100.8 all-gather.4
  114.5 80.5 all-gather.2
  464.8 49.0 all-reduce.2
where the time goes:
time: 529 us; the launch traced here: 523 us
  waiting for transfers between devices  282 us (53%)
  matrix products  84 us (16%)
  local copies, waits for them, and re-layouts  83.7 us (16%)
  other arithmetic  32.5 us (6%)
  starting transfers between devices  27.5 us (5%)
  between operations  14.1 us (3%)
    all_to_all x1, waiting for transfers between devices, local(): lax.all_to_all(dkeys.reshape(peers, per_peer, BLOCK_LEN * width).astype(j...  100 us
    all_gather x1, waiting for transfers between devices, local(): lax.all_gather(w_uk, 'seq', axis=1, tiled=True)  78.3 us
    all_gather x1, waiting for transfers between devices, local(): lax.all_gather(w_uv, 'seq', axis=1, tiled=True)  67.8 us
    unnamed x25, local copies, waits for them, and re-layouts  45.4 us
    convert_element_type x1, other arithmetic, local(): dkeys.reshape(peers, per_peer, BLOCK_LEN * width).astype(jnp.bfloat16)  29.9 us
    convert_element_type x3, local copies, waits for them, and re-layouts, local(): dkeys.reshape(peers, per_peer, BLOCK_LEN * width).astype(jnp.bfloat16)  29.9 us
    psum x1, waiting for transfers between devices, local(): lax.psum(local_grad.astype(jnp.bfloat16), 'grp').astype(jnp.float32)  27.6 us
    dot_general x1, matrix products, local(): jnp.einsum('qht,qhc->tc', dscore, qfull, preferred_element_type=jnp.float32)  18.8 us
  transfers between devices with their start and end apart: 6, of which 5 were waited for; matrix products, arithmetic and copies ran while one was open for 9% of the time, Pallas kernels for 0%

commit v1 on v0

--- a/solution.py
+++ b/solution.py
@@ -8,6 +8,18 @@
 
 
 def local(q_nope, q_rope, cache, w_uk, w_uv, d_out, sel, slot_blocks):
+
+    def drive_shapes(join_dim, arr_in, mesh_dim):
+        return jnp.concatenate(
+            lax.all_to_all(
+                jnp.stack([arr_in for _ in range(lax.axis_size(mesh_dim))]),
+                axis_name=mesh_dim,
+                split_axis=0,
+                concat_axis=0,
+            ),
+            join_dim,
+        )
+
     peers = lax.axis_size("seq")
     queries, heads, nope = q_nope.shape
     rope = q_rope.shape[2]
@@ -19,7 +31,7 @@
     own_blocks = cache.shape[0] // BLOCK_LEN
     scale = 1.0 / math.sqrt(nope + rope)
     gathered_k, gathered_v = (
-        lax.all_gather(w_uk, "seq", axis=1, tiled=True),
+        drive_shapes(1, w_uk, "seq"),
         lax.all_gather(w_uv, "seq", axis=1, tiled=True),
     )
     weight_k = gathered_k.reshape(heads, nope, latent)

time: 529 us -> 599 us (1.13)
  waiting for transfers between devices: 282 us -> 324 us
  blocking collectives: 0 us -> 20.5 us
  local copies, waits for them, and re-layouts: 83.7 us -> 94.2 us
  starting transfers between devices: 27.5 us -> 18.5 us
    all_to_all x1, waiting for transfers between devices: 6.86 us -> 89.6 us  [drive_shapes(): lax.all_to_all(jnp.stack([arr_in for _ in range(lax.axis_size(mesh_dim))]...]
    all_gather x1 -> x0, waiting for transfers between devices: 78.3 us -> none  [local(): lax.all_gather(w_uk, 'seq', axis=1, tiled=True)]
    all_gather x1, waiting for transfers between devices: 67.8 us -> 98.3 us  [local(): lax.all_gather(w_uv, 'seq', axis=1, tiled=True)]
    all_to_all x0 -> x1, blocking collectives: none -> 20.5 us  [local(): lax.all_to_all(wanted, 'seq', split_axis=0, concat_axis=0, tiled=True)]
    another operation x0 -> x2, local copies, waits for them, and re-layouts: none -> 10.9 us  [the longest x1 7.64 us: local(): weight_k = gathered_k.reshape(heads, nope, latent)]
    all_to_all x1, waiting for transfers between devices: 0.01 us -> 7.32 us  [local(): lax.all_to_all(blocks[asked], 'seq', split_axis=0, concat_axis=0, tiled=T...]
    reshape x0 -> x1, local copies, waits for them, and re-layouts: none -> 6.54 us  [drive_shapes(): jnp.concatenate(lax.all_to_all(jnp.stack([arr_in for _ in range(lax.axis_...]
    unnamed x25 -> x24, local copies, waits for them, and re-layouts: 45.4 us -> 39 us
  transfers between devices with their start and end apart: 6 -> 5, of which waited for: 5 -> 5; matrix products, arithmetic and copies ran while one was open for 9% -> 10% of each run, Pallas kernels for 0% -> 0%
where the time goes in v1:
time: 599 us; the launch traced here: 590 us
  waiting for transfers between devices  324 us (54%)
  local copies, waits for them, and re-layouts  94.2 us (16%)
  matrix products  86.3 us (14%)
  other arithmetic  32.5 us (5%)
  blocking collectives  20.5 us (3%)
  starting transfers between devices  18.5 us (3%)
  between operations  14.4 us (2%)
    all_to_all x1, waiting for transfers between devices, local(): lax.all_to_all(dkeys.reshape(peers, per_peer, BLOCK_LEN * width).astype(j...  100 us
    all_gather x1, waiting for transfers between devices, local(): lax.all_gather(w_uv, 'seq', axis=1, tiled=True)  98.3 us
    all_to_all x1, waiting for transfers between devices, drive_shapes(): lax.all_to_all(jnp.stack([arr_in for _ in range(lax.axis_size(mesh_dim))]...  89.6 us
    unnamed x24, local copies, waits for them, and re-layouts  39 us
    convert_element_type x1, other arithmetic, local(): dkeys.reshape(peers, per_peer, BLOCK_LEN * width).astype(jnp.bfloat16)  29.9 us
    convert_element_type x3, local copies, waits for them, and re-layouts, local(): dkeys.reshape(peers, per_peer, BLOCK_LEN * width).astype(jnp.bfloat16)  29.9 us
    psum x1, waiting for transfers between devices, local(): lax.psum(local_grad.astype(jnp.bfloat16), 'grp').astype(jnp.float32)  27.5 us
    all_to_all x1, blocking collectives, local(): lax.all_to_all(wanted, 'seq', split_axis=0, concat_axis=0, tiled=True)  20.5 us
  transfers between devices with their start and end apart: 5, of which 5 were waited for; matrix products, arithmetic and copies ran while one was open for 10% of the time, Pallas kernels for 0%

profile of v1, /device:TPU:8, one launch (start us, length us, event | category | flops | bytes accessed | tf_op | source)
XLA Modules:
  0.0 590.2 jit_solution(8614910462081501529)
XLA Ops:
  8.0 20.5 %all_to_all.24 = s32[64,1,1]{2,1,0:T(1,128)S(1)} all-to-all(s32[64,1,1]{2,1,0:T(1,128)S(1)} %copy.83), channel_id=1, replica_groups=mesh['seq'=64,'grp'=4] {'seq'}, dimensions={0} | all-to-all | bytes 512 | tf_op jit(solution)/shard_map/all_to_all | solution.py:40
  31.8 6.6 %all-to-all-start = ((bf16[64,32,1024]{2,1,0:T(8,128)(2,1)}), bf16[64,32,1024]{2,1,0:T(8,128)(2,1)}, u32[]{:S(2)}, u32[]{:S(2)}) async-start(bf16[64,32,1024]{2,1,0:T(8,128)(2,1)} %stack.2), calls=%async_computation | async-start | bytes 8388608 | tf_op jit(solution)/shard_map/all_to_all | solution.py:14
  45.0 89.6 %all-to-all-done = bf16[64,32,1024]{2,1,0:T(8,128)(2,1)} async-done(((bf16[64,32,1024]{2,1,0:T(8,128)(2,1)}), bf16[64,32,1024]{2,1,0:T(8,128)(2,1)}, u32[]{:S(2)}, u32[]{:S(2)}) %all-to-all-start) | async-done | bytes 4194336 | tf_op jit(solution)/shard_map/all_to_all | solution.py:14
  134.6 5.9 all-to-all-start.2
  141.9 98.3 %all-gather.2.cloned.1.call-done = bf16[32,65536]{1,0:T(8,128)(2,1)} async-done(((bf16[32,1024]{1,0:T(8,128)(2,1)}), bf16[32,65536]{1,0:T(8,128)(2,1)}) %all-gather.2.cloned.1.call-update) | async-done | bytes 4194320 | tf_op jit(solution)/shard_map/all_gather | solution.py:35
  240.2 5.1 copy.104
  245.3 6.5 %copy.79 = bf16[32,64,1024]{2,1,0:T(8,128)(2,1)} copy(bf16[32,64,1024]{2,0,1:T(8,128)(2,1)} %bitcast) | data formatting | bytes 8388608 | tf_op jit(solution)/shard_map/reshape | solution.py:13
  251.9 7.6 %reshape_reshape.3 = bf16[32,128,512]{2,1,0:T(8,128)(2,1)} reshape(bf16[32,64,1024]{2,1,0:T(8,128)(2,1)} %copy.79) | data formatting | bytes 8388608 | tf_op jit(solution)/shard_map/reshape;reshape | solution.py:37
  264.1 7.3 %all-to-all-done.2 = bf16[64,1,64,576]{3,2,1,0:T(8,128)(2,1)} async-done(((bf16[64,1,64,576]{3,2,1,0:T(8,128)(2,1)}), bf16[64,1,64,576]{3,2,1,0:T(8,128)(2,1)}, u32[]{:S(2)}, u32[]{:S(2)}) %all-to-all-start.2) | async-done | bytes 4718624 | tf_op jit(solution)/shard_map/all_to_all | solution.py:42
  271.5 7.9 %fusion.12 = f32[16,32,4096]{2,1,0:T(8,128)} fusion(bf16[4096,576]{1,0:T(8,128)(2,1)} %bitcast.6, bf16[16,32,512]{2,0,1:T(8,128)(2,1)S(1)} %fusion.27), kind=kOutput, calls=%fused_computation.20 | convolution fusion | flops 2147483648 | bytes 13107200 | tf_op jit(solution)/shard_map/qhl,tl->qht/dot_general | solution.py:66
  279.4 10.7 %fusion.50 = (f32[16,32]{1,0:T(8,128)S(1)}, f32[16,32,4096]{2,1,0:T(8,128)}) fusion(pred[16,4096]{1,0:T(8,128)(4,1)S(1)} %broadcast_in_dim.25, bf16[4096,576,1]{1,0,2:T(8,128)(2,1)} %bitcast.7, bf16[16,32,576]{2,0,1:T(8,128)(2,1)S(1)} %pad_maximum_fusion), kind=kOutput, calls=%fused_computation.59 | convolution fusion | flops 2424311808 | bytes 13764608 | tf_op jit(solution)/shard_map/sub | solution.py:55
  290.1 9.2 %convolution_bitcast_fusion = f32[4096,512]{0,1:T(8,128)} fusion(bf16[16,32,512]{2,0,1:T(8,128)(2,1)S(1)} %fusion.27, f32[16,32,4096]{2,1,0:T(8,128)} %get-tuple-element.27, f32[16,32]{1,0:T(8,128)S(1)} %get-tuple-element.26), kind=kOutput, calls=%fused_computation.12 | convolution fusion | flops 2151677952 | bytes 17303552 | tf_op jit(solution)/shard_map/qht,qhl->tl/dot_general | solution.py:75
  299.3 19.0 %fusion.2 = bf16[4096,576]{0,1:T(8,128)(2,1)} fusion(f32[4096,512]{0,1:T(8,128)} %convolution_bitcast_fusion, f32[16,32,4096]{2,1,0:T(8,128)} %fusion.12, bf16[16,32,576]{2,0,1:T(8,128)(2,1)S(1)} %pad_maximum_fusion, f32[16,32,4096]{2,1,0:T(8,128)} %get-tuple-element.27, f32[16,32]{1,0:T(8,128)S(1)} %get-tuple-element.26), kind=kOutput, calls=%fused_computation.5 | convolution fusion | flops 2435322368 | bytes 30476288 | tf_op jit(solution)/shard_map/qht,qhc->tc/dot_general | solution.py:76
  318.3 7.6 %copy.94 = bf16[4096,576]{1,0:T(8,128)(2,1)} copy(bf16[4096,576]{0,1:T(8,128)(2,1)} %fusion.2) | data formatting | bytes 9437184 | tf_op jit(solution)/shard_map/convert_element_type | solution.py:82
  325.9 21.7 %convert_element_type.71 = bf16[64,1,36864]{2,1,0:T(2,128)(2,1)} reshape(bf16[4096,576]{1,0:T(8,128)(2,1)} %copy.94) | data formatting | bytes 9437184 | tf_op jit(solution)/shard_map/convert_element_type | solution.py:82
  348.2 29.9 %reduce.4 = bf16[64,36864]{1,0:T(8,128)(2,1)} reduce(bf16[64,1,36864]{2,1,0:T(2,128)(2,1)} %convert_element_type.71, bf16[]{:T(256)} %broadcast.38), dimensions={1}, to_apply=%convert_element_type.71.reduce_sub_computation | reduce | bytes 9437186 | tf_op jit(solution)/shard_map/convert_element_type | solution.py:82
  378.1 8.3 %reshape.86 = bf16[64,2,18432]{2,1,0:T(2,128)(2,1)} reshape(bf16[64,36864]{1,0:T(8,128)(2,1)} %reduce.4) | data formatting | bytes 9437184
  386.4 5.9 all-to-all-start.3
  392.3 7.0 %fusion.24 = bf16[16,32,512]{2,1,0:T(8,128)(2,1)S(1)} fusion(bf16[4096,576]{1,0:T(8,128)(2,1)} %bitcast.6, f32[16,32,4096]{2,1,0:T(8,128)} %get-tuple-element.27, f32[16,32]{1,0:T(8,128)S(1)} %get-tuple-element.26), kind=kOutput, calls=%fused_computation.26 | convolution fusion | flops 2151940096 | bytes 13109248 | tf_op jit(solution)/shard_map/qht,tl->qhl/dot_general | solution.py:57
  399.3 100.3 %all-to-all-done.3 = bf16[64,2,18432]{2,1,0:T(2,128)(2,1)} async-done(((bf16[64,2,18432]{2,1,0:T(2,128)(2,1)}), bf16[64,2,18432]{2,1,0:T(2,128)(2,1)}, u32[]{:S(2)}, u32[]{:S(2)}) %all-to-all-start.3) | async-done | bytes 4718624 | tf_op jit(solution)/shard_map/all_to_all | solution.py:81
  499.6 20.4 %reshape.87 = bf16[64,1,36864]{2,1,0:T(2,128)(2,1)} reshape(bf16[64,2,18432]{2,1,0:T(2,128)(2,1)} %all-to-all-done.3) | data formatting | bytes 9437184
  520.0 8.8 %convolution_convert_fusion = bf16[16,36864]{1,0:T(8,128)(2,1)S(1)} fusion(bf16[64,1,36864]{2,1,0:T(2,128)(2,1)} %reshape.87, s32[64]{0:T(128)S(1)} %get-tuple-element.24), kind=kOutput, calls=%fused_computation.3 | convolution fusion | flops 76088320 | bytes 5898496 | tf_op jit(solution)/shard_map/dot_general | solution.py:88
  531.2 14.8 %fusion.21 = bf16[16,32,576]{2,1,0:T(8,128)(2,1)S(1)} fusion(bf16[4096,576,1]{1,0,2:T(8,128)(2,1)} %bitcast.7, f32[16,32,4096]{2,1,0:T(8,128)} %fusion.12, f32[16,32,4096]{2,1,0:T(8,128)} %get-tuple-element.27, f32[16,32]{1,0:T(8,128)S(1)} %get-tuple-element.26), kind=kOutput, calls=%fused_computation.25 | convolution fusion | flops 2430898688 | bytes 22087680 | tf_op jit(solution)/shard_map/qht,tc->qhc/dot_general | solution.py:69
  552.9 27.5 %all-reduce.3.cloned.1.call-done = bf16[1024,576]{1,0:T(8,128)(2,1)} async-done(((bf16[1024,576]{1,0:T(8,128)(2,1)}), bf16[1024,576]{1,0:T(8,128)(2,1)}) %all-reduce.3.cloned.1.call-update) | async-done | bytes 1179664 | tf_op jit(solution)/shard_map/psum | solution.py:94
  (42 shorter events, 29.3 us)
Async XLA Ops:
  7.2 255.4 %copy-start = (bf16[16,32,128]{2,1,0:T(8,128)(2,1)S(1)}, bf16[16,32,128]{2,1,0:T(8,128)(2,1)}, u32[]{:S(2)}) copy-start(bf16[16,32,128]{2,1,0:T(8,128)(2,1)} %param.13) | copy-start | bytes 393220
  31.8 6.6 %copy-start.4 = (bf16[1024,576]{0,1:T(8,128)(2,1)S(1)}, bf16[1024,576]{0,1:T(8,128)(2,1)}, u32[]{:S(2)}) copy-start(bf16[1024,576]{0,1:T(8,128)(2,1)} %param.10) | copy-start | bytes 3538948
  31.8 102.8 %all-to-all-start = ((bf16[64,32,1024]{2,1,0:T(8,128)(2,1)}), bf16[64,32,1024]{2,1,0:T(8,128)(2,1)}, u32[]{:S(2)}, u32[]{:S(2)}) async-start(bf16[64,32,1024]{2,1,0:T(8,128)(2,1)} %stack.2), calls=%async_computation | async-start | bytes 8388608 | tf_op jit(solution)/shard_map/all_to_all | solution.py:14
  134.6 6.6 %copy-start.7 = (s32[16,32]{1,0:T(8,128)S(1)}, s32[16,32]{1,0:T(8,128)}, u32[]{:S(2)}) copy-start(s32[16,32]{1,0:T(8,128)} %param.14) | copy-start | bytes 6148
  134.6 7.3 %copy-start.6 = (bf16[16,32,64]{2,1,0:T(8,128)(2,1)S(1)}, bf16[16,32,64]{2,1,0:T(8,128)(2,1)}, u32[]{:S(2)}) copy-start(bf16[16,32,64]{2,1,0:T(8,128)(2,1)} %param.9) | copy-start | bytes 196612
  134.6 136.9 %all-to-all-start.2 = ((bf16[64,1,64,576]{3,2,1,0:T(8,128)(2,1)}), bf16[64,1,64,576]{3,2,1,0:T(8,128)(2,1)}, u32[]{:S(2)}, u32[]{:S(2)}) async-start(bf16[64,1,64,576]{3,2,1,0:T(8,128)(2,1)} %bitcast.44), calls=%async_computation.2 | async-start | bytes 10485760 | tf_op jit(solution)/shard_map/all_to_all | solution.py:42
  140.5 99.7 %all-gather.2.cloned.1.call-start = ((), (), s32[]{:S(2)}) async-start(), calls=%async_computation.4 | async-start | bytes 4259840 | tf_op jit(solution)/shard_map/all_gather | solution.py:35
  251.9 7.7 %copy-start.5 = (bf16[16,32,128]{2,1,0:T(8,128)(2,1)S(1)}, bf16[16,32,128]{2,1,0:T(8,128)(2,1)}, u32[]{:S(2)}) copy-start(bf16[16,32,128]{2,1,0:T(8,128)(2,1)} %param.8) | copy-start | bytes 393220
  259.5 3.5 copy-start.3
  386.4 113.2 %all-to-all-start.3 = ((bf16[64,2,18432]{2,1,0:T(2,128)(2,1)}), bf16[64,2,18432]{2,1,0:T(2,128)(2,1)}, u32[]{:S(2)}, u32[]{:S(2)}) async-start(bf16[64,2,18432]{2,1,0:T(2,128)(2,1)} %reshape.86), calls=%async_computation.3 | async-start | bytes 9437184 | tf_op jit(solution)/shard_map/all_to_all | solution.py:81
  392.3 188.2 %all-reduce.3.cloned.1.call-start = ((), (), s32[]{:S(2)}) async-start(), calls=%async_computation.5 | async-start | bytes 2621440 | tf_op jit(solution)/shard_map/psum | solution.py:94
  546.0 5.0 copy-start.2
  546.7 36.4 %copy-start.1 = (bf16[16,32,128]{2,1,0:T(8,128)(2,1)S(1)}, bf16[16,32,128]{2,1,0:T(8,128)(2,1)}, u32[]{:S(2)}) copy-start(bf16[16,32,128]{2,1,0:T(8,128)(2,1)} %param.13) | copy-start | bytes 393220
Sparse Core Ops, SparseCore 0:
  144.1 96.0 all-gather.1
  531.3 49.0 all-reduce.2
